TPU v7x, 256 devices: a whole 4x4x8 slice. The times are simulated.
256 devices in a mesh: seq: 16 (over y, x), fsdp: 16 (over z, core).
Axes of the slice: x: 4, y: 4, z: 8, core: 2. Of those that a mesh axis runs over, the one named last changes fastest.
Arguments:
- kv_cache: bfloat16 [2, 32, 8192, 1280], P(None, 'fsdp', 'seq'), may hold values from -6 to 6
- keep_flags: int32 [32, 8192], P('fsdp', 'seq'), may hold values from 0 to 1, as said below
- block_weights: float32 [32, 8192], P('fsdp', 'seq'), may hold values from 0.05 to 2
- lengths: int32 [32], P('fsdp'), may hold values from 2048 to 8192, as said below
- token_qkv: bfloat16 [32, 3840], P('fsdp'), may hold values from -10 to 10
- stream: bfloat16 [32, 1280], P('fsdp'), may hold values from -0.59765625 to 0.59765625
- w_out: bfloat16 [1280, 1280], P(None, 'fsdp'), may hold values from -0.15625 to 0.15625
- w_up: bfloat16 [1280, 1280], P(None, 'fsdp'), may hold values from -0.15625 to 0.15625
- w_down: bfloat16 [1280, 1280], P(None, 'fsdp'), may hold values from -0.15625 to 0.15625
- w_qkv: bfloat16 [1280, 3840], P(None, 'fsdp'), may hold values from -0.15625 to 0.15625
- mlp_gain: float32 [1280], replicated, may hold values from 0.1 to 1.9
- next_gain: float32 [1280], replicated, may hold values from 0.1 to 1.9
Outputs:
- packed_cache: bfloat16 [2, 32, 8192, 1280], P(None, 'fsdp', 'seq')
- block_summary: bfloat16 [2, 32, 512, 1280], P(None, 'fsdp', 'seq')
- layer_out: bfloat16 [32, 1280], P('fsdp', 'seq')
- next_qkv: bfloat16 [32, 3840], P('fsdp', 'seq')
Inputs may be any that keep to these rules, and one draw needn't show every extreme that they name: `keep_flags`: in every draw one request keeps all 512 positions of one aligned block of 512 positions. `lengths`: in every draw some request has 8192 filled positions.
All inputs are finite; a program needn't handle non-finite values.
Results may differ from a plain program's by a relative error of at most 0.02.
Values may be sent and summed in bfloat16 or wider, within the bound.
A program may use at most 128 MiB of HBM per device.

v0:
```python
import math
import jax
import jax.numpy as jnp
from jax import lax
from jax.sharding import PartitionSpec as P

H = 16
BLK = 16
neg_fill = -1e30


def combined_all(part, axis, combine):
    gathered = jax.tree.map(lambda a: lax.all_gather(a, axis), part)

    def take(source):
        return jax.tree.map(lambda a: lax.dynamic_index_in_dim(a, source, 0, False), gathered)

    return lax.fori_loop(
        1, lax.axis_size(axis), lambda source, state: combine(state, take(source)), take(0)
    )


def normalize(values, gain):
    wide = values.astype(jnp.float32)
    factor = lax.rsqrt(jnp.mean(wide * wide, axis=-1, keepdims=True) + 1e-06)
    return (wide * factor * gain).astype(jnp.bfloat16)


def combine_parts(first, second):
    peak_a, total_a, accum_a = first
    peak_b, total_b, accum_b = second
    peak = jnp.maximum(peak_a, peak_b)
    factor_a = jnp.exp(peak_a - peak)
    factor_b = jnp.exp(peak_b - peak)
    return (
        peak,
        total_a * factor_a + total_b * factor_b,
        accum_a * factor_a[..., None] + accum_b * factor_b[..., None],
    )


def partial_softmax(queries, keys, values, usable, inv_root):
    scores = (
        jnp.einsum("rhe,rnhe->rhn", queries, keys, preferred_element_type=jnp.float32) * inv_root
    )
    scores = jnp.where(usable[:, None, :], scores, neg_fill)
    peak = jnp.max(scores, axis=-1)
    expo = jnp.where(usable[:, None, :], jnp.exp(scores - peak[..., None]), 0.0)
    total = jnp.sum(expo, axis=-1)
    accum = jnp.einsum("rhn,rnhe->rhe", expo, values, preferred_element_type=jnp.float32)
    return (peak, total, accum)


def split_heads(block):
    return block.reshape(block.shape[:-1] + (H, block.shape[-1] // H))


def body(
    kv_cache,
    keep_flags,
    block_weights,
    lengths,
    token_qkv,
    stream,
    w_out,
    w_up,
    w_down,
    w_qkv,
    mlp_gain,
    next_gain,
):
    seq_count = lax.axis_size("seq")
    seq_here = lax.axis_index("seq")
    reqs = kv_cache.shape[1]
    rows = kv_cache.shape[2]
    width = kv_cache.shape[3]
    head_size = width // H
    inv_root = 1.0 / math.sqrt(head_size)
    position = seq_here * rows + jnp.arange(rows, dtype=jnp.int32)
    in_range = position[None, :] < lengths[:, None]
    kept_rows = in_range & (keep_flags == 1)
    drop_rows = in_range & (keep_flags == 0)
    inclusive = jnp.cumsum(kept_rows.astype(jnp.int32), axis=1)
    held = inclusive[:, -1]
    every = lax.all_gather(held[None, :], "seq", axis=0, tiled=True)
    lower = jnp.arange(seq_count, dtype=jnp.int32)[:, None] < seq_here
    before = jnp.sum(jnp.where(lower, every, 0), axis=0)
    blocks = rows // BLK
    drop_weight = jnp.where(drop_rows, block_weights, 0.0).reshape(reqs, blocks, BLK)
    weight_total = jnp.sum(drop_weight, axis=-1)
    drop_count = jnp.sum(drop_rows.reshape(reqs, blocks, BLK).astype(jnp.int32), axis=-1)
    sums = jnp.einsum(
        "rbk,crbkd->crbd",
        drop_weight,
        kv_cache.reshape(2, reqs, blocks, BLK, width),
        preferred_element_type=jnp.float32,
        precision=lax.Precision.HIGHEST,
    )
    block_summary = (sums / jnp.maximum(weight_total, 1.0)[None, :, :, None]).astype(jnp.bfloat16)
    queries = split_heads(token_qkv[:, :width])
    own_keys = split_heads(token_qkv[:, width : 2 * width])
    own_values = split_heads(token_qkv[:, 2 * width :])
    slot = rows // seq_count
    target = jnp.arange(seq_count, dtype=jnp.int32)
    offset = jnp.mod(target[:, None] - before[None, :], seq_count)
    sent = (held[None, :] - offset + seq_count - 1) // seq_count
    wanted = offset[:, :, None] + seq_count * jnp.arange(slot, dtype=jnp.int32)[None, None, :]
    local_rank = inclusive - 1
    wanted_r = jnp.transpose(wanted, (1, 0, 2))
    pick_send = (
        kept_rows[:, None, None, :] & (local_rank[:, None, None, :] == wanted_r[:, :, :, None])
    ).astype(jnp.bfloat16)
    outgoing = jnp.einsum(
        "rtsp,crpd->ctrsd", pick_send, kv_cache, preferred_element_type=jnp.float32
    ).astype(jnp.bfloat16)
    incoming, arrived = (
        lax.all_to_all(outgoing, "seq", split_axis=1, concat_axis=1, tiled=True),
        lax.all_to_all(sent[None], "seq", split_axis=1, concat_axis=1, tiled=True),
    )
    counts_in = arrived[0]
    ends = jnp.cumsum(counts_in, axis=0)
    starts = ends - counts_in
    filled = ends[-1]
    local_rows = jnp.arange(rows, dtype=jnp.int32)
    slot_index = jnp.arange(slot, dtype=jnp.int32)
    starts_r = starts.T
    counts_r = counts_in.T
    valid_slot = slot_index[None, None, :] < counts_r[:, :, None]
    dest_row = starts_r[:, :, None] + slot_index[None, None, :]
    pick_recv = (
        valid_slot[:, None, :, :] & (dest_row[:, None, :, :] == local_rows[None, :, None, None])
    ).astype(jnp.bfloat16)
    packed_cache = jnp.einsum(
        "rlts,ctrsd->crld", pick_recv, incoming, preferred_element_type=jnp.float32
    ).astype(jnp.bfloat16)
    present = local_rows[None, :] < filled[:, None]
    row_part = partial_softmax(
        queries, split_heads(packed_cache[0]), split_heads(packed_cache[1]), present, inv_root
    )
    summary_part = partial_softmax(
        queries,
        split_heads(block_summary[0]),
        split_heads(block_summary[1]),
        drop_count > 0,
        inv_root,
    )
    peak, total, accum = combined_all(combine_parts(row_part, summary_part), "seq", combine_parts)
    own_score = (
        jnp.einsum("rhe,rhe->rh", queries, own_keys, preferred_element_type=jnp.float32) * inv_root
    )
    top_score = jnp.maximum(peak, own_score)
    factor_old = jnp.exp(peak - top_score)
    factor_own = jnp.exp(own_score - top_score)
    attended = (
        accum * factor_old[..., None] + factor_own[..., None] * own_values.astype(jnp.float32)
    ) / (total * factor_old + factor_own)[..., None]
    attended = attended.reshape(reqs, width).astype(jnp.bfloat16)
    fsdp_here = lax.axis_index("fsdp")

    def widen(columns):
        return lax.all_gather(columns, "fsdp", axis=1, tiled=True)

    def own_columns(full, count):
        return lax.dynamic_slice_in_dim(full, fsdp_here * count, count, 1)

    attn_all, stream_all = (
        lax.all_gather(attended, "fsdp", axis=0, tiled=True),
        lax.all_gather(stream, "fsdp", axis=0, tiled=True),
    )
    mid_cols = own_columns(stream_all, w_out.shape[1]).astype(jnp.float32) + jnp.dot(
        attn_all, w_out, preferred_element_type=jnp.float32
    )
    mid = widen(mid_cols.astype(jnp.bfloat16))
    hidden = widen(
        jax.nn.silu(
            jnp.dot(normalize(mid, mlp_gain), w_up, preferred_element_type=jnp.float32)
        ).astype(jnp.bfloat16)
    )
    out_cols = own_columns(mid, w_down.shape[1]).astype(jnp.float32) + jnp.dot(
        hidden, w_down, preferred_element_type=jnp.float32
    )
    layer_all = widen(out_cols.astype(jnp.bfloat16))
    qkv_all = widen(
        jnp.dot(normalize(layer_all, next_gain), w_qkv, preferred_element_type=jnp.float32).astype(
            jnp.bfloat16
        )
    )
    layer_rows = lax.dynamic_slice_in_dim(layer_all, fsdp_here * reqs, reqs, 0)
    qkv_rows = lax.dynamic_slice_in_dim(qkv_all, fsdp_here * reqs, reqs, 0)
    layer_width = width // seq_count
    qkv_width = 3 * width // seq_count
    layer_out = lax.dynamic_slice_in_dim(layer_rows, seq_here * layer_width, layer_width, 1)
    next_qkv = lax.dynamic_slice_in_dim(qkv_rows, seq_here * qkv_width, qkv_width, 1)
    return (packed_cache, block_summary, layer_out, next_qkv)


def solution(mesh):
    placed = (
        P(None, "fsdp", "seq", None),
        P("fsdp", "seq"),
        P("fsdp", "seq"),
        P("fsdp"),
        P("fsdp", None),
        P("fsdp", None),
        P(None, "fsdp"),
        P(None, "fsdp"),
        P(None, "fsdp"),
        P(None, "fsdp"),
        P(),
        P(),
    )
    return jax.shard_map(
        body,
        mesh=mesh,
        in_specs=placed,
        out_specs=(
            P(None, "fsdp", "seq", None),
            P(None, "fsdp", "seq", None),
            P("fsdp", "seq"),
            P("fsdp", "seq"),
        ),
        check_vma=False,
    )
```

profile of v0, /device:TPU:1, one launch (start us, length us, event | category | flops | bytes accessed | tf_op | source)
XLA Modules:
  0.0 290.0 jit_solution(1825323752103344393)
XLA Ops:
  0.7 0.8 fusion.76
  2.8 1.3 dynamic-slice
  4.8 13.9 %all-reduce = s32[32]{0:T(128)S(1)} all-reduce(s32[32]{0:T(128)S(1)} %bitcast_dynamic-update-slice_fusion), channel_id=2, replica_groups=mesh['seq'=16,'fsdp'=16] {'seq'}, use_global_device_ids=true, to_apply=%add | all-reduce | flops 32 | bytes 256
  19.6 3.5 %all-to-all-start.1 = ((s32[1,16,2]{2,0,1:T(1,128)}), s32[1,16,2]{2,0,1:T(1,128)S(1)}, u32[]{:S(2)}, u32[]{:S(2)}) async-start(s32[1,16,2]{2,0,1:T(1,128)} %and_select_fusion), calls=%async_computation.1 | async-start | bytes 16384 | tf_op jit(solution)/shard_map/all_to_all | solution.py:118
  23.2 5.4 %fusion.7 = bf16[2,16,2,32,1280]{4,3,1,0,2:T(8,128)(2,1)S(1)} fusion(s32[2,16,32]{2,1,0:T(8,128)S(1)} %broadcast_add_fusion, s32[2,512]{1,0:T(2,128)S(1)} %broadcast_add_fusion.1, pred[2,512]{1,0:T(4,128)(4,1)S(1)} %get-tuple-element.236, bf16[2,2,512,1280]{3,2,1,0:T(8,128)(2,1)} %param.14), kind=kOutput, calls=%fused_computation.15 | convolution fusion | flops 2688024576 | bytes 10494976 | tf_op jit(solution)/shard_map/rtsp,crpd->ctrsd/dot_general | solution.py:113
  28.6 2.8 copy.45
  31.5 6.8 %all-to-all-start = ((bf16[2,16,2,32,1280]{4,3,0,2,1:T(8,128)(2,1)}), bf16[2,16,2,32,1280]{4,3,0,2,1:T(8,128)(2,1)}, u32[]{:S(2)}, u32[]{:S(2)}) async-start(bf16[2,16,2,32,1280]{4,3,0,2,1:T(8,128)(2,1)} %copy.45), calls=%async_computation | async-start | bytes 10485760 | tf_op jit(solution)/shard_map/all_to_all | solution.py:117
  38.8 4.8 %fusion.5 = f32[2,32,1,2,1280]{4,2,3,1,0:T(1,128)S(1)} fusion(f32[2,32,16,1,1]{2,3,4,1,0:T(1,128)S(1)} %bitcast.193, bf16[2,2,32,16,1280]{4,3,2,1,0:T(8,128)(2,1)} %bitcast.190), kind=kOutput, calls=%fused_computation.13 | convolution fusion | flops 31457280 | bytes 5902336 | tf_op jit(solution)/shard_map/rbk,crbkd->crbd/dot_general | solution.py:92
  43.7 0.7 copy-done.2
  45.6 24.9 %all-gather.2 = bf16[16,2,1280]{2,1,0:T(2,128)(2,1)S(1)} all-gather(bf16[1,2,1280]{2,1,0:T(2,128)(2,1)S(1)} %bitcast.202), channel_id=1, replica_groups=mesh['seq'=16,'fsdp'=16] {'fsdp'}, dimensions={0}, use_global_device_ids=true | all-gather | bytes 87040 | tf_op jit(solution)/shard_map/all_gather | solution.py:168
  71.6 0.8 fusion.75
  72.3 0.8 fusion.29
  73.7 30.8 %all-to-all-done = bf16[2,16,2,32,1280]{4,3,0,2,1:T(8,128)(2,1)} async-done(((bf16[2,16,2,32,1280]{4,3,0,2,1:T(8,128)(2,1)}), bf16[2,16,2,32,1280]{4,3,0,2,1:T(8,128)(2,1)}, u32[]{:S(2)}, u32[]{:S(2)}) %all-to-all-start) | async-done | bytes 5242912 | tf_op jit(solution)/shard_map/all_to_all | solution.py:117
  104.5 5.7 %fusion.12 = bf16[2,2,1280,512,1]{3,2,1,0,4:T(8,128)(2,1)S(1)} fusion(bf16[2,16,2,32,1280]{4,3,0,2,1:T(8,128)(2,1)} %all-to-all-done, s32[2,16,32]{2,0,1:T(2,128)S(1)} %iota_add_fusion, pred[2,16,32]{2,0,1:T(4,128)(4,1)S(1)} %iota_compare_fusion.1), kind=kOutput, calls=%fused_computation.19 | convolution fusion | flops 2685403136 | bytes 10490880 | tf_op jit(solution)/shard_map/rlts,ctrsd->crld/dot_general | solution.py:133
  110.9 1.9 copy-done.1
  113.4 0.7 fusion.51
  114.7 0.7 fusion.52
  115.4 7.9 %copy.55 = bf16[2,2,512,1280]{3,2,1,0:T(8,128)(2,1)} copy(bf16[2,2,512,1280]{2,3,1,0:T(8,128)(2,1)} %bitcast.188) | data formatting | bytes 10485760
  123.3 1.5 fusion.49
  124.9 0.8 multiply_add_fusion
  125.7 18.9 %all-gather.1 = f32[32,16,80]{2,1,0:T(8,128)S(1)} all-gather(f32[2,16,80]{2,1,0:T(8,128)S(1)} %multiply_add_fusion), channel_id=3, replica_groups=mesh['seq'=16,'fsdp'=16] {'seq'}, dimensions={0}, use_global_device_ids=true | all-gather | bytes 174080 | tf_op jit(solution)/shard_map/all_gather | solution.py:13
  145.3 16.3 %all_gather.38 = f32[16,2,16]{2,1,0:T(2,128)S(1)} all-gather(f32[1,2,16]{2,1,0:T(2,128)S(1)} %get-tuple-element.239), channel_id=1, replica_groups=mesh['seq'=16,'fsdp'=16] {'seq'}, dimensions={0}, use_global_device_ids=true | all-gather | bytes 2176 | tf_op jit(solution)/shard_map/all_gather | solution.py:13
  161.6 16.5 %all_gather.37 = f32[16,2,16]{2,1,0:T(2,128)S(1)} all-gather(f32[1,2,16]{2,1,0:T(2,128)S(1)} %get-tuple-element.240), channel_id=1, replica_groups=mesh['seq'=16,'fsdp'=16] {'seq'}, dimensions={0}, use_global_device_ids=true | all-gather | bytes 2176 | tf_op jit(solution)/shard_map/all_gather | solution.py:13
  178.1 1.5 while.19
  179.6 0.7 multiply_add_fusion.1
  180.5 41.5 %all-gather.3 = bf16[16,2,1280]{2,1,0:T(2,128)(2,1)S(1)} all-gather(bf16[1,2,1280]{2,1,0:T(2,128)(2,1)S(1)} %reshape.375), channel_id=1, replica_groups=mesh['seq'=16,'fsdp'=16] {'fsdp'}, dimensions={0}, use_global_device_ids=true | all-gather | bytes 87040 | tf_op jit(solution)/shard_map/all_gather | solution.py:167
  222.3 14.8 %all-gather.4 = bf16[16,80,32]{1,2,0:T(8,128)(2,1)S(1)} all-gather(bf16[1,80,32]{1,2,0:T(8,128)(2,1)S(1)} %fusion.21), channel_id=1, replica_groups=mesh['seq'=16,'fsdp'=16] {'fsdp'}, dimensions={0}, use_global_device_ids=true | all-gather | bytes 87040 | tf_op jit(solution)/shard_map/all_gather | solution.py:161
  237.4 1.2 fusion.57
  238.7 16.1 %all-gather.5 = bf16[16,80,32]{1,2,0:T(8,128)(2,1)S(1)} all-gather(bf16[1,80,32]{1,2,0:T(8,128)(2,1)S(1)} %fusion.57), channel_id=1, replica_groups=mesh['seq'=16,'fsdp'=16] {'fsdp'}, dimensions={0}, use_global_device_ids=true | all-gather | bytes 87040 | tf_op jit(solution)/shard_map/all_gather | solution.py:161
  255.0 1.1 fusion.20
  256.2 14.8 %all-gather.6 = bf16[16,80,32]{1,2,0:T(8,128)(2,1)S(1)} all-gather(bf16[1,80,32]{1,2,0:T(8,128)(2,1)S(1)} %fusion.20), channel_id=1, replica_groups=mesh['seq'=16,'fsdp'=16] {'fsdp'}, dimensions={0}, use_global_device_ids=true | all-gather | bytes 87040 | tf_op jit(solution)/shard_map/all_gather | solution.py:161
  271.6 16.6 %all-gather.7 = bf16[16,240,32]{1,2,0:T(8,128)(2,1)S(1)} all-gather(bf16[1,240,32]{1,2,0:T(8,128)(2,1)S(1)} %fusion.17), channel_id=1, replica_groups=mesh['seq'=16,'fsdp'=16] {'fsdp'}, dimensions={0}, use_global_device_ids=true | all-gather | bytes 261120 | tf_op jit(solution)/shard_map/all_gather | solution.py:161
  (128 shorter events, 13.1 us)
Async XLA Ops:
  0.6 270.7 %copy-start = (bf16[1280,240]{0,1:T(8,128)(2,1)S(1)}, bf16[1280,240]{0,1:T(8,128)(2,1)}, u32[]{:S(2)}) copy-start(bf16[1280,240]{0,1:T(8,128)(2,1)} %param.23) | copy-start | bytes 1843204
  19.6 11.9 %all-to-all-start.1 = ((s32[1,16,2]{2,0,1:T(1,128)}), s32[1,16,2]{2,0,1:T(1,128)S(1)}, u32[]{:S(2)}, u32[]{:S(2)}) async-start(s32[1,16,2]{2,0,1:T(1,128)} %and_select_fusion), calls=%async_computation.1 | async-start | bytes 16384 | tf_op jit(solution)/shard_map/all_to_all | solution.py:118
  31.5 6.8 %copy-start.10 = (f32[2,512]{1,0:T(2,128)S(1)}, f32[2,512]{1,0:T(2,128)}, u32[]{:S(2)}) copy-start(f32[2,512]{1,0:T(2,128)} %param.16) | copy-start | bytes 12292
  31.5 7.0 %copy-start.7 = (bf16[2,3840]{1,0:T(2,128)(2,1)S(1)}, bf16[2,3840]{1,0:T(2,128)(2,1)}, u32[]{:S(2)}) copy-start(bf16[2,3840]{1,0:T(2,128)(2,1)} %param.18) | copy-start | bytes 46084
  31.5 73.0 %all-to-all-start = ((bf16[2,16,2,32,1280]{4,3,0,2,1:T(8,128)(2,1)}), bf16[2,16,2,32,1280]{4,3,0,2,1:T(8,128)(2,1)}, u32[]{:S(2)}, u32[]{:S(2)}) async-start(bf16[2,16,2,32,1280]{4,3,0,2,1:T(8,128)(2,1)} %copy.45), calls=%async_computation | async-start | bytes 10485760 | tf_op jit(solution)/shard_map/all_to_all | solution.py:117
  38.3 7.3 %copy-start.9 = (bf16[2,1280]{1,0:T(2,128)(2,1)S(1)}, bf16[2,1280]{1,0:T(2,128)(2,1)}, u32[]{:S(2)}) copy-start(bf16[2,1280]{1,0:T(2,128)(2,1)} %param.19) | copy-start | bytes 15364
  43.7 0.7 copy-start.2
  71.6 38.6 %copy-start.4 = (f32[2,16]{1,0:T(2,128)}, f32[2,16]{1,0:T(2,128)S(1)}, u32[]{:S(2)}) copy-start(f32[2,16]{1,0:T(2,128)S(1)} %fusion.60) | copy-start | bytes 388
  110.5 2.3 copy-start.1
  110.5 3.5 %copy-start.5 = (f32[2,16]{1,0:T(2,128)S(1)}, f32[2,16]{1,0:T(2,128)}, u32[]{:S(2)}) copy-start(f32[2,16]{1,0:T(2,128)} %copy-done.4) | copy-start | bytes 388
  115.4 29.2 %copy-start.6 = (f32[2,16]{1,0:T(2,128)S(1)}, f32[2,16]{1,0:T(2,128)}, u32[]{:S(2)}) copy-start(f32[2,16]{1,0:T(2,128)} %copy-done.4) | copy-start | bytes 388
  115.4 106.6 %copy-start.3 = (bf16[1280,80]{0,1:T(8,128)(2,1)S(1)}, bf16[1280,80]{0,1:T(8,128)(2,1)}, u32[]{:S(2)}) copy-start(bf16[1280,80]{0,1:T(8,128)(2,1)} %param.20) | copy-start | bytes 614404
  123.3 148.0 %copy-start.8 = (f32[1280]{0:T(1024)S(1)}, f32[1280]{0:T(1024)}, u32[]{:S(2)}) copy-start(f32[1280]{0:T(1024)} %param.25) | copy-start | bytes 15364
where the time goes:
time: 291 us; the launch traced here: 290 us
  blocking collectives  194 us (67%)
  waiting for transfers between devices  30.8 us (11%)
  matrix products  21.6 us (7%)
  local copies, waits for them, and re-layouts  20.2 us (7%)
  other arithmetic  11 us (4%)
  starting transfers between devices  10.2 us (4%)
    all_gather x4, blocking collectives, widen(): return lax.all_gather(columns, 'fsdp', axis=1, tiled=True)  62.3 us
    all_gather x3, blocking collectives, combined_all(): gathered = jax.tree.map(lambda a: lax.all_gather(a, axis), part)  51.7 us
    all_gather x1, blocking collectives, body(): lax.all_gather(attended, 'fsdp', axis=0, tiled=True)  41.5 us
    all_to_all x1, waiting for transfers between devices, body(): lax.all_to_all(outgoing, 'seq', split_axis=1, concat_axis=1, tiled=True)  30.8 us
    all_gather x1, blocking collectives, body(): lax.all_gather(stream, 'fsdp', axis=0, tiled=True)  24.9 us
    unnamed x1, blocking collectives  13.9 us
    unnamed x35, local copies, waits for them, and re-layouts  13.1 us
    all_to_all x1, starting transfers between devices, body(): lax.all_to_all(outgoing, 'seq', split_axis=1, concat_axis=1, tiled=True)  6.77 us
  transfers between devices with their start and end apart: 2, of which 1 were waited for; matrix products, arithmetic and copies ran while one was open for 6% of the time, Pallas kernels for 0%

commit v1 on v0

--- a/solution.py
+++ b/solution.py
@@ -7,6 +7,12 @@
 H = 16
 BLK = 16
 neg_fill = -1e30
+
+
+def gather_from_all(x, axis, dim):
+    size = lax.axis_size(axis)
+    repeats = [size if d == dim else 1 for d in range(x.ndim)]
+    return lax.all_to_all(jnp.tile(x, repeats), axis, split_axis=dim, concat_axis=dim, tiled=True)
 
 
 def combined_all(part, axis, combine):
@@ -158,7 +164,7 @@
     fsdp_here = lax.axis_index("fsdp")
 
     def widen(columns):
-        return lax.all_gather(columns, "fsdp", axis=1, tiled=True)
+        return gather_from_all(columns, "fsdp", 1)
 
     def own_columns(full, count):
         return lax.dynamic_slice_in_dim(full, fsdp_here * count, count, 1)

time: 291 us -> 265 us (0.911)
  blocking collectives: 194 us -> 168 us
  waiting for transfers between devices: 30.8 us -> 36 us
  other arithmetic: 11 us -> 5.97 us
  starting transfers between devices: 10.2 us -> 13.7 us
  matrix products: 21.6 us -> 18.4 us
    all_gather x4 -> x0, blocking collectives: 62.3 us -> none  [widen(): return lax.all_gather(columns, 'fsdp', axis=1, tiled=True)]
    all_to_all x0 -> x3, blocking collectives: none -> 36 us  [gather_from_all(): lax.all_to_all(jnp.tile(x, repeats), axis, split_axis=dim, concat_axis=di...]
    all_to_all x0 -> x1, starting transfers between devices: none -> 3.43 us  [gather_from_all(): lax.all_to_all(jnp.tile(x, repeats), axis, split_axis=dim, concat_axis=di...]
    unnamed x35 -> x31, local copies, waits for them, and re-layouts: 13.1 us -> 11.5 us
  transfers between devices with their start and end apart: 2 -> 3, of which waited for: 1 -> 2; matrix products, arithmetic and copies ran while one was open for 6% -> 9% of each run, Pallas kernels for 0% -> 0%
where the time goes in v1:
time: 265 us; the launch traced here: 264 us
  blocking collectives  168 us (63%)
  waiting for transfers between devices  36 us (14%)
  local copies, waits for them, and re-layouts  20.4 us (8%)
  matrix products  18.4 us (7%)
  starting transfers between devices  13.7 us (5%)
  other arithmetic  5.97 us (2%)
    all_gather x3, blocking collectives, combined_all(): gathered = jax.tree.map(lambda a: lax.all_gather(a, axis), part)  51.9 us
    all_gather x1, blocking collectives, body(): lax.all_gather(attended, 'fsdp', axis=0, tiled=True)  41.4 us
    all_to_all x3, blocking collectives, gather_from_all(): lax.all_to_all(jnp.tile(x, repeats), axis, split_axis=dim, concat_axis=di...  36 us
    all_to_all x1, waiting for transfers between devices, body(): lax.all_to_all(outgoing, 'seq', split_axis=1, concat_axis=1, tiled=True)  33.3 us
    all_gather x1, blocking collectives, body(): lax.all_gather(stream, 'fsdp', axis=0, tiled=True)  24.9 us
    unnamed x1, blocking collectives  13.9 us
    unnamed x31, local copies, waits for them, and re-layouts  11.5 us
    all_to_all x1, starting transfers between devices, body(): lax.all_to_all(outgoing, 'seq', split_axis=1, concat_axis=1, tiled=True)  6.77 us
  transfers between devices with their start and end apart: 3, of which 2 were waited for; matrix products, arithmetic and copies ran while one was open for 9% of the time, Pallas kernels for 0%

profile of v1, /device:TPU:1, one launch (start us, length us, event | category | flops | bytes accessed | tf_op | source)
XLA Modules:
  0.0 264.2 jit_solution(11118597917049394386)
XLA Ops:
  0.7 0.8 fusion.59
  1.5 0.6 reduce-window.6
  2.8 1.3 dynamic-slice
  4.8 13.9 %all-reduce = s32[32]{0:T(128)S(1)} all-reduce(s32[32]{0:T(128)S(1)} %bitcast_dynamic-update-slice_fusion), channel_id=2, replica_groups=mesh['seq'=16,'fsdp'=16] {'seq'}, use_global_device_ids=true, to_apply=%add | all-reduce | flops 32 | bytes 256
  18.9 0.7 and_select_fusion
  19.6 3.5 %all-to-all-start.1 = ((s32[1,16,2]{2,0,1:T(1,128)}), s32[1,16,2]{2,0,1:T(1,128)S(1)}, u32[]{:S(2)}, u32[]{:S(2)}) async-start(s32[1,16,2]{2,0,1:T(1,128)} %and_select_fusion), calls=%async_computation.1 | async-start | bytes 16384 | tf_op jit(solution)/shard_map/all_to_all | solution.py:124
  23.2 5.4 %fusion.9 = bf16[2,16,2,32,1280]{4,3,1,0,2:T(8,128)(2,1)S(1)} fusion(s32[2,16,32]{2,1,0:T(8,128)S(1)} %broadcast_add_fusion, s32[2,512]{1,0:T(2,128)S(1)} %broadcast_add_fusion.1, pred[2,512]{1,0:T(4,128)(4,1)S(1)} %get-tuple-element.240, bf16[2,2,512,1280]{3,2,1,0:T(8,128)(2,1)} %param.14), kind=kOutput, calls=%fused_computation.17 | convolution fusion | flops 2688024576 | bytes 10494976 | tf_op jit(solution)/shard_map/rtsp,crpd->ctrsd/dot_general | solution.py:119
  28.6 2.8 %copy.51 = bf16[2,16,2,32,1280]{4,3,0,2,1:T(8,128)(2,1)} copy(bf16[2,16,2,32,1280]{4,3,1,0,2:T(8,128)(2,1)S(1)} %fusion.9) | data formatting | bytes 10485760 | tf_op jit(solution)/shard_map/convert_element_type | solution.py:121
  31.5 6.8 %all-to-all-start = ((bf16[2,16,2,32,1280]{4,3,0,2,1:T(8,128)(2,1)}), bf16[2,16,2,32,1280]{4,3,0,2,1:T(8,128)(2,1)}, u32[]{:S(2)}, u32[]{:S(2)}) async-start(bf16[2,16,2,32,1280]{4,3,0,2,1:T(8,128)(2,1)} %copy.51), calls=%async_computation | async-start | bytes 10485760 | tf_op jit(solution)/shard_map/all_to_all | solution.py:123
  38.8 4.8 %fusion.5 = f32[2,32,1,2,1280]{4,2,3,1,0:T(1,128)S(1)} fusion(f32[2,32,16,1,1]{2,3,4,1,0:T(1,128)S(1)} %bitcast.148, bf16[2,2,32,16,1280]{4,3,2,1,0:T(8,128)(2,1)} %bitcast.145), kind=kOutput, calls=%fused_computation.13 | convolution fusion | flops 31457280 | bytes 5902336 | tf_op jit(solution)/shard_map/rbk,crbkd->crbd/dot_general | solution.py:98
  43.7 0.4 reshape_squeeze.13
  44.3 0.4 reshape_squeeze.15
  44.9 24.9 %all-gather.2 = bf16[16,2,1280]{2,1,0:T(2,128)(2,1)S(1)} all-gather(bf16[1,2,1280]{2,1,0:T(2,128)(2,1)S(1)} %bitcast.157), channel_id=1, replica_groups=mesh['seq'=16,'fsdp'=16] {'fsdp'}, dimensions={0}, use_global_device_ids=true | all-gather | bytes 87040 | tf_op jit(solution)/shard_map/all_gather | solution.py:174
  71.2 33.3 %all-to-all-done = bf16[2,16,2,32,1280]{4,3,0,2,1:T(8,128)(2,1)} async-done(((bf16[2,16,2,32,1280]{4,3,0,2,1:T(8,128)(2,1)}), bf16[2,16,2,32,1280]{4,3,0,2,1:T(8,128)(2,1)}, u32[]{:S(2)}, u32[]{:S(2)}) %all-to-all-start) | async-done | bytes 5242912 | tf_op jit(solution)/shard_map/all_to_all | solution.py:123
  104.5 5.7 %fusion.7 = bf16[2,2,1280,512,1]{3,2,0,1,4:T(8,128)(2,1)S(1)} fusion(bf16[2,16,2,32,1280]{4,3,0,2,1:T(8,128)(2,1)} %all-to-all-done, s32[2,16,32]{2,0,1:T(2,128)S(1)} %iota_add_fusion, pred[2,16,32]{2,0,1:T(4,128)(4,1)S(1)} %iota_compare_fusion.1), kind=kOutput, calls=%fused_computation.15 | convolution fusion | flops 2685403136 | bytes 10490880 | tf_op jit(solution)/shard_map/rlts,ctrsd->crld/dot_general | solution.py:139
  110.9 1.9 copy-done.1
  112.9 0.4 fusion.64
  113.7 0.8 fusion.37
  114.5 18.9 %all-gather.1 = f32[32,16,80]{2,1,0:T(8,128)S(1)} all-gather(f32[2,16,80]{2,1,0:T(8,128)S(1)} %multiply_add_fusion), channel_id=3, replica_groups=mesh['seq'=16,'fsdp'=16] {'seq'}, dimensions={0}, use_global_device_ids=true | all-gather | bytes 174080 | tf_op jit(solution)/shard_map/all_gather | solution.py:19
  133.5 16.3 %all_gather.26 = f32[16,2,16]{2,1,0:T(2,128)S(1)} all-gather(f32[1,2,16]{2,1,0:T(2,128)S(1)} %get-tuple-element.243), channel_id=1, replica_groups=mesh['seq'=16,'fsdp'=16] {'seq'}, dimensions={0}, use_global_device_ids=true | all-gather | bytes 2176 | tf_op jit(solution)/shard_map/all_gather | solution.py:19
  149.8 16.7 %all_gather.25 = f32[16,2,16]{2,1,0:T(2,128)S(1)} all-gather(f32[1,2,16]{2,1,0:T(2,128)S(1)} %get-tuple-element.244), channel_id=1, replica_groups=mesh['seq'=16,'fsdp'=16] {'seq'}, dimensions={0}, use_global_device_ids=true | all-gather | bytes 2176 | tf_op jit(solution)/shard_map/all_gather | solution.py:19
  166.5 1.5 while.19
  168.2 41.4 %all-gather.3 = bf16[16,2,1280]{2,1,0:T(2,128)(2,1)S(1)} all-gather(bf16[1,2,1280]{2,1,0:T(2,128)(2,1)S(1)} %reshape.403), channel_id=1, replica_groups=mesh['seq'=16,'fsdp'=16] {'fsdp'}, dimensions={0}, use_global_device_ids=true | all-gather | bytes 87040 | tf_op jit(solution)/shard_map/all_gather | solution.py:173
  209.8 12.8 %all_to_all.46 = bf16[32,16,80]{2,0,1:T(8,128)(2,1)S(1)} all-to-all(bf16[32,16,80]{2,0,1:T(8,128)(2,1)S(1)} %tile.8), channel_id=1, replica_groups=mesh['seq'=16,'fsdp'=16] {'fsdp'}, dimensions={1} | all-to-all | bytes 163840 | tf_op jit(solution)/shard_map/all_to_all | solution.py:15
  223.3 11.6 %all_to_all.47 = bf16[32,16,80]{2,0,1:T(8,128)(2,1)S(1)} all-to-all(bf16[32,16,80]{2,0,1:T(8,128)(2,1)S(1)} %tile.9), channel_id=1, replica_groups=mesh['seq'=16,'fsdp'=16] {'fsdp'}, dimensions={1} | all-to-all | bytes 163840 | tf_op jit(solution)/shard_map/all_to_all | solution.py:15
  235.3 11.6 %all_to_all.48 = bf16[32,16,80]{2,0,1:T(8,128)(2,1)S(1)} all-to-all(bf16[32,16,80]{2,0,1:T(8,128)(2,1)S(1)} %tile.10), channel_id=1, replica_groups=mesh['seq'=16,'fsdp'=16] {'fsdp'}, dimensions={1} | all-to-all | bytes 163840 | tf_op jit(solution)/shard_map/all_to_all | solution.py:15
  247.6 0.8 tile.11
  248.4 3.4 %all-to-all-start.5 = ((bf16[32,16,240]{2,0,1:T(8,128)(2,1)}), bf16[32,16,240]{2,0,1:T(8,128)(2,1)S(1)}, u32[]{:S(2)}, u32[]{:S(2)}) async-start(bf16[32,16,240]{2,0,1:T(8,128)(2,1)} %tile.11), calls=%async_computation.5 | async-start | bytes 524288 | tf_op jit(solution)/shard_map/all_to_all | solution.py:15
  251.9 7.9 %copy.60 = bf16[2,2,512,1280]{3,2,1,0:T(8,128)(2,1)} copy(bf16[2,2,512,1280]{2,3,0,1:T(8,128)(2,1)} %bitcast.143) | data formatting | bytes 10485760
  259.7 0.6 dynamic_slice.60
  260.3 2.7 %all-to-all-done.5 = bf16[32,16,240]{2,0,1:T(8,128)(2,1)S(1)} async-done(((bf16[32,16,240]{2,0,1:T(8,128)(2,1)}), bf16[32,16,240]{2,0,1:T(8,128)(2,1)S(1)}, u32[]{:S(2)}, u32[]{:S(2)}) %all-to-all-start.5) | async-done | bytes 245792 | tf_op jit(solution)/shard_map/all_to_all | solution.py:15
  263.5 0.7 dynamic_slice.61
  (133 shorter events, 8.8 us)
Async XLA Ops:
  0.6 246.7 %copy-start = (bf16[1280,240]{0,1:T(8,128)(2,1)S(1)}, bf16[1280,240]{0,1:T(8,128)(2,1)}, u32[]{:S(2)}) copy-start(bf16[1280,240]{0,1:T(8,128)(2,1)} %param.23) | copy-start | bytes 1843204
  19.6 11.9 %all-to-all-start.1 = ((s32[1,16,2]{2,0,1:T(1,128)}), s32[1,16,2]{2,0,1:T(1,128)S(1)}, u32[]{:S(2)}, u32[]{:S(2)}) async-start(s32[1,16,2]{2,0,1:T(1,128)} %and_select_fusion), calls=%async_computation.1 | async-start | bytes 16384 | tf_op jit(solution)/shard_map/all_to_all | solution.py:124
  31.5 6.8 %copy-start.8 = (f32[2,512]{1,0:T(2,128)S(1)}, f32[2,512]{1,0:T(2,128)}, u32[]{:S(2)}) copy-start(f32[2,512]{1,0:T(2,128)} %param.16) | copy-start | bytes 12292
  31.5 7.0 %copy-start.5 = (bf16[2,3840]{1,0:T(2,128)(2,1)S(1)}, bf16[2,3840]{1,0:T(2,128)(2,1)}, u32[]{:S(2)}) copy-start(bf16[2,3840]{1,0:T(2,128)(2,1)} %param.18) | copy-start | bytes 46084
  31.5 73.0 %all-to-all-start = ((bf16[2,16,2,32,1280]{4,3,0,2,1:T(8,128)(2,1)}), bf16[2,16,2,32,1280]{4,3,0,2,1:T(8,128)(2,1)}, u32[]{:S(2)}, u32[]{:S(2)}) async-start(bf16[2,16,2,32,1280]{4,3,0,2,1:T(8,128)(2,1)} %copy.51), calls=%async_computation | async-start | bytes 10485760 | tf_op jit(solution)/shard_map/all_to_all | solution.py:123
  38.3 6.6 %copy-start.7 = (bf16[2,1280]{1,0:T(2,128)(2,1)S(1)}, bf16[2,1280]{1,0:T(2,128)(2,1)}, u32[]{:S(2)}) copy-start(bf16[2,1280]{1,0:T(2,128)(2,1)} %param.19) | copy-start | bytes 15364
  43.7 66.5 %copy-start.2 = (bf16[2,2,32,1280]{3,2,1,0:T(8,128)(2,1)}, bf16[2,2,32,1280]{3,2,1,0:T(8,128)(2,1)S(1)}, u32[]{:S(2)}) copy-start(bf16[2,2,32,1280]{3,2,1,0:T(8,128)(2,1)S(1)} %fusion.26) | copy-start | bytes 983044
  110.5 2.3 copy-start.1
  112.8 96.7 %copy-start.3 = (bf16[1280,80]{0,1:T(8,128)(2,1)S(1)}, bf16[1280,80]{0,1:T(8,128)(2,1)}, u32[]{:S(2)}) copy-start(bf16[1280,80]{0,1:T(8,128)(2,1)} %param.20) | copy-start | bytes 614404
  112.8 110.1 %copy-start.9 = (bf16[1280,80]{0,1:T(8,128)(2,1)S(1)}, bf16[1280,80]{0,1:T(8,128)(2,1)}, u32[]{:S(2)}) copy-start(bf16[1280,80]{0,1:T(8,128)(2,1)} %param.21) | copy-start | bytes 614404
  112.8 110.1 %copy-start.10 = (f32[1280]{0:T(1024)S(1)}, f32[1280]{0:T(1024)}, u32[]{:S(2)}) copy-start(f32[1280]{0:T(1024)} %param.24) | copy-start | bytes 15364
  112.8 122.3 %copy-start.4 = (bf16[1280,80]{0,1:T(8,128)(2,1)S(1)}, bf16[1280,80]{0,1:T(8,128)(2,1)}, u32[]{:S(2)}) copy-start(bf16[1280,80]{0,1:T(8,128)(2,1)} %param.22) | copy-start | bytes 614404
  112.9 134.5 %copy-start.6 = (f32[1280]{0:T(1024)S(1)}, f32[1280]{0:T(1024)}, u32[]{:S(2)}) copy-start(f32[1280]{0:T(1024)} %param.25) | copy-start | bytes 15364
  248.4 14.6 %all-to-all-start.5 = ((bf16[32,16,240]{2,0,1:T(8,128)(2,1)}), bf16[32,16,240]{2,0,1:T(8,128)(2,1)S(1)}, u32[]{:S(2)}, u32[]{:S(2)}) async-start(bf16[32,16,240]{2,0,1:T(8,128)(2,1)} %tile.11), calls=%async_computation.5 | async-start | bytes 524288 | tf_op jit(solution)/shard_map/all_to_all | solution.py:15
